TPU v7x, 256 devices: a whole 4x4x8 slice. The times are simulated.
256 devices in a mesh: firm: 16 (over y_lo, z), tm: 16 (over x, y_hi, core).
Axes of the slice: x: 4, y: 4 (y_hi: 2, y_lo: 2; y = y_hi * 2 + y_lo), z: 8, core: 2. Of those that a mesh axis runs over, the one named last changes fastest.
Arguments:
- features: bfloat16 [8192, 32, 128], P('firm', 'tm'), may hold values from -6 to 6
- cotangent: bfloat16 [8192, 32, 128], P('firm', 'tm'), may hold values from -6 to 6
- tiles: bfloat16 [64, 64, 128, 128], P('firm'), may hold values from -0.125 to 0.125
- mask: int32 [64, 64], P('firm'), may hold values 0 or 1
- w_prev: bfloat16 [2, 128, 256], replicated, may hold values from -0.375 to 0.375
- w_cur: bfloat16 [2, 128, 256], replicated, may hold values from -0.375 to 0.375
- w_self: bfloat16 [2, 128, 128], replicated, may hold values from -0.5 to 0.5
- w_nbr: bfloat16 [2, 128, 128], replicated, may hold values from -0.5 to 0.5
- dilations: int32 [2], replicated, may hold values from 1 to 2, as said below
Outputs:
- grad_features: float32 [8192, 32, 128], P('firm', 'tm')
- grad_prev: float32 [2, 128, 256], replicated
- grad_cur: float32 [2, 128, 256], replicated
- grad_self: float32 [2, 128, 128], replicated
- grad_nbr: float32 [2, 128, 128], replicated
Inputs may be any that keep to these rules, and one draw needn't show every extreme that they name: `dilations`: each layer's dilation lies between 1 and 2; some layer has dilation 1 and some layer has dilation 2.
All inputs are finite; a program needn't handle non-finite values. No bound on the sum of `mask` on one device may be relied on, other than what follows from the above.
Results may differ from a plain program's by a relative error of at most 0.007.
Values may be sent and summed in bfloat16 or wider, within the bound.
No kernel may reach another device: no remote copies, remote signals or barrier semaphores. Data moves between devices by JAX's collectives and lax.ppermute only.
A program may use at most 128 MiB of HBM per device.

v0:
```python
import jax
import jax.numpy as jnp
from jax import lax
from jax.sharding import PartitionSpec as P

L = 2


def shifted(array, axis, by):
    peers = lax.axis_size(axis)
    pairs = [(i, i + by) for i in range(peers) if 0 <= i + by < peers]
    return lax.ppermute(array, axis, pairs)


def earlier_time_days(hidden_state, dilation_factor):
    time_days = hidden_state.shape[1]
    prior = shifted(hidden_state, "tm", 1)
    paired_terms = jnp.concatenate([prior, hidden_state], axis=1)
    return lax.dynamic_slice_in_dim(paired_terms, time_days - dilation_factor, time_days, 1)


def later_time_days(reverse_flow, dilation_factor):
    time_days = reverse_flow.shape[1]
    following = shifted(reverse_flow, "tm", -1)
    paired_terms = jnp.concatenate([reverse_flow, following], axis=1)
    return lax.dynamic_slice_in_dim(paired_terms, dilation_factor, time_days, 1)


def folder(matrix, piece):
    return jnp.dot(matrix, piece, preferred_element_type=jnp.float32)


def per_device(features, cotangent, tiles, mask, w_prev, w_cur, w_self, w_nbr, dilations):
    rows, time_days, width = features.shape
    blocks_local, blocks_all, block_size, _ = tiles.shape
    all_firms = blocks_all * block_size
    masked = tiles * mask.astype(tiles.dtype)[:, :, None, None]
    row_matrix = masked.transpose(0, 2, 1, 3).reshape(rows, all_firms)
    saved = []
    hidden_state = features
    for layer_index in range(L):
        dilation_factor = dilations[layer_index]
        previous_state = earlier_time_days(hidden_state, dilation_factor)
        pre = jnp.dot(
            previous_state.reshape(-1, width),
            w_prev[layer_index],
            preferred_element_type=jnp.float32,
        )
        pre = pre + jnp.dot(
            hidden_state.reshape(-1, width), w_cur[layer_index], preferred_element_type=jnp.float32
        )
        filt = pre[:, :width]
        gate = pre[:, width:]
        gated = (jnp.tanh(filt) * jax.nn.sigmoid(gate)).astype(jnp.bfloat16)
        diffused = folder(
            row_matrix,
            lax.all_gather(gated.reshape(rows, time_days * width), "firm", axis=0, tiled=True),
        ).astype(jnp.bfloat16)
        mixed = jnp.dot(gated, w_self[layer_index], preferred_element_type=jnp.float32)
        mixed = mixed + jnp.dot(
            diffused.reshape(-1, width), w_nbr[layer_index], preferred_element_type=jnp.float32
        )
        saved.append((hidden_state, previous_state, filt, gate, gated, diffused))
        hidden_state = (
            hidden_state.astype(jnp.float32) + mixed.reshape(rows, time_days, width)
        ).astype(jnp.bfloat16)
    gradient_value = cotangent.astype(jnp.float32)
    outs_prev, outs_cur, outs_self, outs_nbr = ([], [], [], [])
    for layer_index in reversed(range(L)):
        hidden_state, previous_state, filt, gate, gated, diffused = saved[layer_index]
        dilation_factor = dilations[layer_index]
        gzb = gradient_value.astype(jnp.bfloat16).reshape(-1, width)
        outs_self.append(jnp.dot(gated.T, gzb, preferred_element_type=jnp.float32))
        outs_nbr.append(
            jnp.dot(diffused.reshape(-1, width).T, gzb, preferred_element_type=jnp.float32)
        )
        gdiff = jnp.dot(gzb, w_nbr[layer_index].T, preferred_element_type=jnp.float32).astype(
            jnp.bfloat16
        )
        gdiff_rows = gdiff.reshape(rows, time_days * width)
        spread = lax.psum_scatter(
            lax.dot_general(
                row_matrix, gdiff_rows, (((0,), (0,)), ((), ())), preferred_element_type=jnp.float32
            ),
            "firm",
            scatter_dimension=0,
            tiled=True,
        )
        ggated = jnp.dot(
            gzb, w_self[layer_index].T, preferred_element_type=jnp.float32
        ) + spread.reshape(-1, width)
        tanh_filt = jnp.tanh(filt)
        sig_gate = jax.nn.sigmoid(gate)
        gpre = jnp.concatenate(
            [
                ggated * sig_gate * (1.0 - tanh_filt * tanh_filt),
                ggated * tanh_filt * sig_gate * (1.0 - sig_gate),
            ],
            axis=1,
        ).astype(jnp.bfloat16)
        outs_cur.append(
            jnp.dot(hidden_state.reshape(-1, width).T, gpre, preferred_element_type=jnp.float32)
        )
        outs_prev.append(
            jnp.dot(previous_state.reshape(-1, width).T, gpre, preferred_element_type=jnp.float32)
        )
        reverse_flow = jnp.dot(
            gpre, w_prev[layer_index].T, preferred_element_type=jnp.float32
        ).reshape(rows, time_days, width)
        direct_path = jnp.dot(
            gpre, w_cur[layer_index].T, preferred_element_type=jnp.float32
        ).reshape(rows, time_days, width)
        gradient_value = (
            gradient_value + direct_path + later_time_days(reverse_flow, dilation_factor)
        )
    sums = lax.psum(
        (
            jnp.stack(outs_prev[::-1]),
            jnp.stack(outs_cur[::-1]),
            jnp.stack(outs_self[::-1]),
            jnp.stack(outs_nbr[::-1]),
        ),
        ("firm", "tm"),
    )
    factor = 1.0 / jnp.sqrt(jnp.float32(all_firms * time_days * lax.axis_size("tm")))
    return (gradient_value, sums[0] * factor, sums[1] * factor, sums[2] * factor, sums[3] * factor)


def solution(mesh):
    in_specs = (
        P("firm", "tm", None),
        P("firm", "tm", None),
        P("firm", None, None, None),
        P("firm", None),
        P(),
        P(),
        P(),
        P(),
        P(),
    )
    out_specs = (P("firm", "tm", None), P(), P(), P(), P())
    return jax.shard_map(
        per_device, mesh=mesh, in_specs=in_specs, out_specs=out_specs, check_vma=False
    )
```

profile of v0, /device:TPU:97, one launch (start us, length us, event | category | flops | bytes accessed | tf_op | source)
XLA Modules:
  0.0 658.3 jit_solution(12701526937728373321)
XLA Ops:
  7.2 5.4 collective-permute-start
  12.6 1.3 fusion.67
  15.2 1.2 fusion.39
  16.4 1.9 fusion.29
  18.4 1.2 convolution_add_fusion.1
  21.3 7.2 %multiply_bitcast_fusion = bf16[4,128,64,128]{3,1,2,0:T(8,128)(2,1)} fusion(bf16[4,64,128,128]{3,2,1,0:T(8,128)(2,1)} %param.11, bf16[4,64]{1,0:T(4,128)(2,1)S(1)} %convert_element_type.41), kind=kLoop, calls=%fused_computation.8 | loop fusion | flops 4194304 | bytes 16777728 | tf_op jit(solution)/shard_map/transpose | solution.py:38
  28.6 12.1 %copy.22 = bf16[4,128,64,128]{3,2,1,0:T(8,128)(2,1)} copy(bf16[4,128,64,128]{3,1,2,0:T(8,128)(2,1)} %multiply_bitcast_fusion) | data formatting | bytes 16777216 | tf_op jit(solution)/shard_map/transpose | solution.py:38
  41.0 24.6 %fusion.6 = f32[8192,256]{1,0:T(8,128)} fusion(bf16[512,256]{1,0:T(8,128)(2,1)S(1)} %reshape.86, bf16[64,8,64,128]{3,2,1,0:T(8,128)(2,1)} %bitcast.124), kind=kOutput, calls=%fused_computation.6 | convolution fusion | flops 2147483648 | bytes 17039360 | tf_op jit(solution)/shard_map/dot_general | solution.py:82
  66.7 19.3 %all-gather.3.cloned.1.call-done = bf16[8192,256]{1,0:T(8,128)(2,1)} async-done(((bf16[512,256]{1,0:T(8,128)(2,1)}), bf16[8192,256]{1,0:T(8,128)(2,1)}) %all-gather.3.cloned.1.call-update) | async-done | bytes 4194320 | tf_op jit(solution)/shard_map/all_gather | solution.py:57
  86.1 9.3 %fusion.13 = bf16[512,256]{1,0:T(8,128)(2,1)S(1)} fusion(bf16[8192,256]{1,0:T(8,128)(2,1)} %all-gather.3.cloned.1.call-done, bf16[64,8,64,128]{3,2,1,0:T(8,128)(2,1)} %bitcast.125), kind=kOutput, calls=%fused_computation.23 | convolution fusion | flops 2147614720 | bytes 12845056 | tf_op jit(solution)/shard_map/dot_general | solution.py:30
  95.9 14.7 %collective-permute-start.1 = (bf16[512,2,128]{2,1,0:T(2,128)(2,1)S(1)}, bf16[512,2,128]{2,1,0:T(2,128)(2,1)S(1)}, u32[]{:S(2)}, u32[]{:S(2)}) collective-permute-start(bf16[512,2,128]{2,1,0:T(2,128)(2,1)S(1)} %add_convert_fusion), channel_id=1, source_target_pairs={{0,1},{1,2},{2,3},{3,4},{4,5},{5,6},{6,7},{7,8},{8,9},{9,10},{10,1... | collective-permute-start | bytes 786440 | tf_op jit(solution)/shard_map/ppermute | solution.py:12
  112.3 1.7 collective-permute-done.1
  116.0 82.7 %reduce-scatter.3.cloned.1.call-done = f32[512,256]{1,0:T(8,128)} async-done(((f32[8192,256]{1,0:T(8,128)}), f32[512,256]{1,0:T(8,128)}) %reduce-scatter.3.cloned.1.call-update) | async-done | bytes 524304 | tf_op jit(solution)/shard_map/reduce_scatter | solution.py:81
  198.7 1.9 reshape.87
  200.6 2.4 multiply_convert_fusion.3
  202.9 1.8 reshape.98
  207.1 2.8 collective-permute-start.2
  211.9 7.5 %collective-permute-done.2 = f32[512,2,128]{2,0,1:T(8,128)} collective-permute-done((f32[512,2,128]{2,0,1:T(8,128)S(1)}, f32[512,2,128]{2,0,1:T(8,128)}, u32[]{:S(2)}, u32[]{:S(2)}) %collective-permute-start.2) | collective-permute-done | bytes 524320 | tf_op jit(solution)/shard_map/ppermute | solution.py:12
  219.3 2.2 fusion.68
  222.9 24.2 %fusion.2 = f32[8192,256]{1,0:T(8,128)} fusion(bf16[512,256]{1,0:T(8,128)(2,1)S(1)} %reshape.96, bf16[64,8,64,128]{3,2,1,0:T(8,128)(2,1)} %bitcast.126), kind=kOutput, calls=%fused_computation.2 | convolution fusion | flops 2147483648 | bytes 17039360 | tf_op jit(solution)/shard_map/dot_general | solution.py:82
  248.3 1.9 convolution_bitcast_fusion
  250.2 1.9 convolution_bitcast_fusion.2
  253.3 16.1 %all-gather.5.cloned.1.call-done = bf16[8192,256]{1,0:T(8,128)(2,1)} async-done(((bf16[512,256]{1,0:T(8,128)(2,1)}), bf16[8192,256]{1,0:T(8,128)(2,1)}) %all-gather.5.cloned.1.call-update) | async-done | bytes 4194320 | tf_op jit(solution)/shard_map/all_gather | solution.py:57
  269.4 9.3 %fusion.16 = bf16[512,256]{1,0:T(8,128)(2,1)S(1)} fusion(bf16[8192,256]{1,0:T(8,128)(2,1)} %all-gather.5.cloned.1.call-done, bf16[64,8,64,128]{3,2,1,0:T(8,128)(2,1)} %bitcast.127), kind=kOutput, calls=%fused_computation.24 | convolution fusion | flops 2147614720 | bytes 12845056 | tf_op jit(solution)/shard_map/dot_general | solution.py:30
  279.7 101.9 %reduce-scatter.5.cloned.1.call-done = f32[512,256]{1,0:T(8,128)} async-done(((f32[8192,256]{1,0:T(8,128)}), f32[512,256]{1,0:T(8,128)}) %reduce-scatter.5.cloned.1.call-update) | async-done | bytes 524304 | tf_op jit(solution)/shard_map/reduce_scatter | solution.py:81
  382.7 1.2 multiply_convert_fusion.1
  384.5 1.6 pad_maximum_fusion.7
  387.2 2.7 collective-permute-start.3
  391.8 254.4 %all-reduce.3.cloned.1.call-done = (f32[2,128,256]{2,1,0:T(8,128)}, f32[2,128,256]{2,1,0:T(8,128)}, f32[2,128,128]{2,1,0:T(8,128)}, f32[2,128,128]{2,1,0:T(8,128)}) async-done(((f32[2,128,256]{2,1,0:T(8,128)}, f32[2,128,256]{2,1,0:T(8,128)}, f32[2,128,128]{2,1,0:T(8,128)}, f32[2,128,128]{2,1,0:T(8,128)}), (f32[2,128,256]{2,1,0:T(8,128)}, f32[2,128,256]{2,1,0:T(8,128)}, f32[2,128,128]{2,1,0:T(8,128)}, ...) | async-done | bytes 786448 | tf_op jit(solution)/shard_map/psum | solution.py:116
  646.3 1.7 broadcast_multiply_fusion.2
  647.9 1.9 broadcast_multiply_fusion
  650.1 1.2 copy.29
  (75 shorter events, 16.2 us)
Async XLA Ops:
  7.2 78.9 %all-gather.3.cloned.1.call-start = ((), (), s32[]{:S(2)}) async-start(), calls=%async_computation.3 | async-start | bytes 4456448 | tf_op jit(solution)/shard_map/all_gather | solution.py:57
  7.2 9.2 %collective-permute-start = (bf16[512,2,128]{2,1,0:T(2,128)(2,1)}, bf16[512,2,128]{2,1,0:T(2,128)(2,1)S(1)}, u32[]{:S(2)}, u32[]{:S(2)}) collective-permute-start(bf16[512,2,128]{2,1,0:T(2,128)(2,1)} %param.9), channel_id=1, source_target_pairs={{0,1},{1,2},{2,3},{3,4},{4,5},{5,6},{6,7},{7,8},{8,9},{9,10},{10,1... | collective-permute-start | bytes 786440 | tf_op jit(solution)/shard_map/ppermute | solution.py:12
  18.4 1.2 copy-start.3
  20.6 178.1 %reduce-scatter.3.cloned.1.call-start = ((), (), s32[]{:S(2)}) async-start(), calls=%async_computation.2 | async-start | bytes 8912896 | tf_op jit(solution)/shard_map/reduce_scatter | solution.py:81
  28.6 12.1 %copy-start = (bf16[512,2,128]{2,1,0:T(2,128)(2,1)S(1)}, bf16[512,2,128]{2,1,0:T(2,128)(2,1)}, u32[]{:S(2)}) copy-start(bf16[512,2,128]{2,1,0:T(2,128)(2,1)} %param.10) | copy-start | bytes 786436
  28.6 12.1 %copy-start.12 = (bf16[2,128,128]{2,1,0:T(8,128)(2,1)S(1)}, bf16[2,128,128]{2,1,0:T(8,128)(2,1)}, u32[]{:S(2)}) copy-start(bf16[2,128,128]{2,1,0:T(8,128)(2,1)} %param.16) | copy-start | bytes 196612
  65.6 0.8 copy-start.14
  65.7 203.7 %all-gather.5.cloned.1.call-start = ((), (), s32[]{:S(2)}) async-start(), calls=%async_computation.5 | async-start | bytes 4456448 | tf_op jit(solution)/shard_map/all_gather | solution.py:57
  66.7 29.0 %copy-start.1 = (bf16[512,2,128]{2,1,0:T(2,128)(2,1)S(1)}, bf16[512,2,128]{2,1,0:T(2,128)(2,1)}, u32[]{:S(2)}) copy-start(bf16[512,2,128]{2,1,0:T(2,128)(2,1)} %param.9) | copy-start | bytes 786436
  66.7 45.3 %copy-start.9 = (bf16[2,128,256]{2,1,0:T(8,128)(2,1)S(1)}, bf16[2,128,256]{2,1,0:T(8,128)(2,1)}, u32[]{:S(2)}) copy-start(bf16[2,128,256]{2,1,0:T(8,128)(2,1)} %param.14) | copy-start | bytes 393220
  66.7 49.0 %copy-start.8 = (bf16[2,128,256]{2,1,0:T(8,128)(2,1)S(1)}, bf16[2,128,256]{2,1,0:T(8,128)(2,1)}, u32[]{:S(2)}) copy-start(bf16[2,128,256]{2,1,0:T(8,128)(2,1)} %param.13) | copy-start | bytes 393220
  95.9 18.0 %collective-permute-start.1 = (bf16[512,2,128]{2,1,0:T(2,128)(2,1)S(1)}, bf16[512,2,128]{2,1,0:T(2,128)(2,1)S(1)}, u32[]{:S(2)}, u32[]{:S(2)}) collective-permute-start(bf16[512,2,128]{2,1,0:T(2,128)(2,1)S(1)} %add_convert_fusion), channel_id=1, source_target_pairs={{0,1},{1,2},{2,3},{3,4},{4,5},{5,6},{6,7},{7,8},{8,9},{9,10},{10,1... | collective-permute-start | bytes 786440 | tf_op jit(solution)/shard_map/ppermute | solution.py:12
  115.0 0.7 copy-start.5
  204.7 176.9 %reduce-scatter.5.cloned.1.call-start = ((), (), s32[]{:S(2)}) async-start(), calls=%async_computation.4 | async-start | bytes 8912896 | tf_op jit(solution)/shard_map/reduce_scatter | solution.py:81
  207.1 12.2 %collective-permute-start.2 = (f32[512,2,128]{2,0,1:T(8,128)S(1)}, f32[512,2,128]{2,0,1:T(8,128)}, u32[]{:S(2)}, u32[]{:S(2)}) collective-permute-start(f32[512,2,128]{2,0,1:T(8,128)S(1)} %fusion.33), channel_id=1, source_target_pairs={{1,0},{2,1},{3,2},{4,3},{5,4},{6,5},{7,6},{8,7},{9,8},{10,9},{11,1... | collective-permute-start | bytes 1572872 | tf_op jit(solution)/shard_map/ppermute | solution.py:12
  247.1 1.0 copy-start.7
  247.1 1.2 copy-start.11
  247.1 3.1 copy-start.6
  247.1 399.1 %all-reduce.3.cloned.1.call-start = ((), (), s32[]{:S(2)}) async-start(), calls=%async_computation.6 | async-start | bytes 1572864 | tf_op jit(solution)/shard_map/psum | solution.py:116
  253.3 130.9 %copy-start.4 = (bf16[512,2,128]{2,1,0:T(2,128)(2,1)S(1)}, bf16[512,2,128]{2,1,0:T(2,128)(2,1)}, u32[]{:S(2)}) copy-start(bf16[512,2,128]{2,1,0:T(2,128)(2,1)} %copy-done.3) | copy-start | bytes 786436
  278.7 371.1 %copy-start.2 = (f32[512,2,128]{2,0,1:T(8,128)S(1)}, f32[512,2,128]{2,0,1:T(8,128)}, u32[]{:S(2)}) copy-start(f32[512,2,128]{2,0,1:T(8,128)} %get-tuple-element.27) | copy-start | bytes 1572868
  278.7 371.1 %copy-start.10 = (bf16[2,128,256]{2,1,0:T(8,128)(2,1)S(1)}, bf16[2,128,256]{2,1,0:T(8,128)(2,1)}, u32[]{:S(2)}) copy-start(bf16[2,128,256]{2,1,0:T(8,128)(2,1)} %param.14) | copy-start | bytes 393220
  279.7 106.4 %copy-start.13 = (f32[1,128,256]{2,1,0:T(8,128)S(1)}, f32[1,128,256]{2,1,0:T(8,128)}, u32[]{:S(2)}) copy-start(f32[1,128,256]{2,1,0:T(8,128)} %convolution_bitcast_fusion.2) | copy-start | bytes 393220
  387.2 262.6 %collective-permute-start.3 = (f32[512,2,128]{2,0,1:T(8,128)S(1)}, f32[512,2,128]{2,0,1:T(8,128)S(1)}, u32[]{:S(2)}, u32[]{:S(2)}) collective-permute-start(f32[512,2,128]{2,0,1:T(8,128)S(1)} %fusion.30), channel_id=1, source_target_pairs={{1,0},{2,1},{3,2},{4,3},{5,4},{6,5},{7,6},{8,7},{9,8},{10,9},{11,1... | collective-permute-start | bytes 1572872 | tf_op jit(solution)/shard_map/ppermute | solution.py:12
Sparse Core Ops, SparseCore 0:
  20.7 65.2 all-gather.2
  88.6 110.0 reduce-scatter.2
  204.8 64.4 all-gather.4
  271.8 109.7 reduce-scatter.4
  387.9 258.2 all-reduce.2
where the time goes:
time: 669 us; the launch traced here: 658 us
  waiting for transfers between devices  484 us (72%)
  matrix products  83.9 us (13%)
  starting transfers between devices  26.1 us (4%)
  local copies, waits for them, and re-layouts  25.1 us (4%)
  between operations  21 us (3%)
  other arithmetic  18.5 us (3%)
    psum x1, waiting for transfers between devices, per_device(): lax.psum((jnp.stack(outs_prev[::-1]), jnp.stack(outs_cur[::-1]), jnp.stac...  254 us
    reduce_scatter x2, waiting for transfers between devices, per_device(): lax.psum_scatter(lax.dot_general(row_matrix, gdiff_rows, (((0,), (0,)), (...  185 us
    dot_general x2, matrix products, per_device(): lax.dot_general(row_matrix, gdiff_rows, (((0,), (0,)), ((), ())), preferr...  48.8 us
    all_gather x2, waiting for transfers between devices, per_device(): lax.all_gather(gated.reshape(rows, time_days * width), 'firm', axis=0, ti...  35.4 us
    ppermute x4, starting transfers between devices, shifted(): return lax.ppermute(array, axis, pairs)  25.6 us
    dot_general x2, matrix products, folder(): return jnp.dot(matrix, piece, preferred_element_type=jnp.float32)  18.6 us
  transfers between devices with their start and end apart: 9, of which 7 were waited for; matrix products, arithmetic and copies ran while one was open for 16% of the time, Pallas kernels for 0%

commit v1 on v0

--- a/solution.py
+++ b/solution.py
@@ -114,13 +114,16 @@
             gradient_value + direct_path + later_time_days(reverse_flow, dilation_factor)
         )
     sums = lax.psum(
-        (
-            jnp.stack(outs_prev[::-1]),
-            jnp.stack(outs_cur[::-1]),
-            jnp.stack(outs_self[::-1]),
-            jnp.stack(outs_nbr[::-1]),
+        lax.psum(
+            (
+                jnp.stack(outs_prev[::-1]),
+                jnp.stack(outs_cur[::-1]),
+                jnp.stack(outs_self[::-1]),
+                jnp.stack(outs_nbr[::-1]),
+            ),
+            "tm",
         ),
-        ("firm", "tm"),
+        "firm",
     )
     factor = 1.0 / jnp.sqrt(jnp.float32(all_firms * time_days * lax.axis_size("tm")))
     return (gradient_value, sums[0] * factor, sums[1] * factor, sums[2] * factor, sums[3] * factor)

time: 669 us -> 697 us (1.042)
  the two profiles are of different devices: /device:TPU:97 before, /device:TPU:2 now
where the time goes in v1:
time: 697 us; the launch traced here: 686 us
  waiting for transfers between devices  523 us (75%)
  matrix products  83.9 us (12%)
  local copies, waits for them, and re-layouts  27 us (4%)
  between operations  21 us (3%)
  other arithmetic  19.4 us (3%)
  starting transfers between devices  12.4 us (2%)
    reduce_scatter x2, waiting for transfers between devices, per_device(): lax.psum_scatter(lax.dot_general(row_matrix, gdiff_rows, (((0,), (0,)), (...  165 us
    psum x1, waiting for transfers between devices, per_device(): lax.psum(lax.psum((jnp.stack(outs_prev[::-1]), jnp.stack(outs_cur[::-1]),...  145 us
    psum x1, waiting for transfers between devices, per_device(): lax.psum((jnp.stack(outs_prev[::-1]), jnp.stack(outs_cur[::-1]), jnp.stac...  131 us
    all_gather x2, waiting for transfers between devices, per_device(): lax.all_gather(gated.reshape(rows, time_days * width), 'firm', axis=0, ti...  62.3 us
    dot_general x2, matrix products, per_device(): lax.dot_general(row_matrix, gdiff_rows, (((0,), (0,)), ((), ())), preferr...  48.8 us
    ppermute x4, waiting for transfers between devices, shifted(): return lax.ppermute(array, axis, pairs)  19.7 us
    dot_general x2, matrix products, folder(): return jnp.dot(matrix, piece, preferred_element_type=jnp.float32)  18.6 us
  transfers between devices with their start and end apart: 10, of which 9 were waited for; matrix products, arithmetic and copies ran while one was open for 16% of the time, Pallas kernels for 0%

profile of v1, /device:TPU:2, one launch (start us, length us, event | category | flops | bytes accessed | tf_op | source)
XLA Modules:
  0.0 686.3 jit_solution(8876560272324278944)
XLA Ops:
  7.2 1.9 collective-permute-start
  9.1 1.3 fusion.67
  11.6 1.2 fusion.39
  12.8 4.7 collective-permute-done
  17.5 1.9 fusion.29
  22.4 7.3 %multiply_bitcast_fusion = bf16[4,128,64,128]{3,1,2,0:T(8,128)(2,1)} fusion(bf16[4,64,128,128]{3,2,1,0:T(8,128)(2,1)} %param.11, bf16[4,64]{1,0:T(4,128)(2,1)S(1)} %convert_element_type.41), kind=kLoop, calls=%fused_computation.8 | loop fusion | flops 4194304 | bytes 16777728 | tf_op jit(solution)/shard_map/transpose | solution.py:38
  29.7 12.1 %copy.22 = bf16[4,128,64,128]{3,2,1,0:T(8,128)(2,1)} copy(bf16[4,128,64,128]{3,1,2,0:T(8,128)(2,1)} %multiply_bitcast_fusion) | data formatting | bytes 16777216 | tf_op jit(solution)/shard_map/transpose | solution.py:38
  42.1 24.6 %fusion.6 = f32[8192,256]{1,0:T(8,128)} fusion(bf16[512,256]{1,0:T(8,128)(2,1)S(1)} %reshape.86, bf16[64,8,64,128]{3,2,1,0:T(8,128)(2,1)} %bitcast.124), kind=kOutput, calls=%fused_computation.6 | convolution fusion | flops 2147483648 | bytes 17039360 | tf_op jit(solution)/shard_map/dot_general | solution.py:82
  67.8 32.2 %all-gather.3.cloned.1.call-done = bf16[8192,256]{1,0:T(8,128)(2,1)} async-done(((bf16[512,256]{1,0:T(8,128)(2,1)}), bf16[8192,256]{1,0:T(8,128)(2,1)}) %all-gather.3.cloned.1.call-update) | async-done | bytes 4194320 | tf_op jit(solution)/shard_map/all_gather | solution.py:57
  100.1 9.3 %fusion.13 = bf16[512,256]{1,0:T(8,128)(2,1)S(1)} fusion(bf16[8192,256]{1,0:T(8,128)(2,1)} %all-gather.3.cloned.1.call-done, bf16[64,8,64,128]{3,2,1,0:T(8,128)(2,1)} %bitcast.125), kind=kOutput, calls=%fused_computation.23 | convolution fusion | flops 2147614720 | bytes 12845056 | tf_op jit(solution)/shard_map/dot_general | solution.py:30
  110.0 1.9 collective-permute-start.1
  113.5 10.4 %collective-permute-done.1 = bf16[512,2,128]{2,1,0:T(2,128)(2,1)S(1)} collective-permute-done((bf16[512,2,128]{2,1,0:T(2,128)(2,1)S(1)}, bf16[512,2,128]{2,1,0:T(2,128)(2,1)S(1)}, u32[]{:S(2)}, u32[]{:S(2)}) %collective-permute-start.1) | collective-permute-done | bytes 262176 | tf_op jit(solution)/shard_map/ppermute | solution.py:12
  125.8 75.5 %reduce-scatter.3.cloned.1.call-done = f32[512,256]{1,0:T(8,128)} async-done(((f32[8192,256]{1,0:T(8,128)}), f32[512,256]{1,0:T(8,128)}) %reduce-scatter.3.cloned.1.call-update) | async-done | bytes 524304 | tf_op jit(solution)/shard_map/reduce_scatter | solution.py:81
  201.3 1.9 reshape.87
  203.2 2.4 multiply_convert_fusion.3
  205.6 1.7 reshape.98
  209.7 4.0 collective-permute-start.2
  215.7 4.6 collective-permute-done.2
  220.2 2.2 fusion.68
  223.8 24.2 %fusion.2 = f32[8192,256]{1,0:T(8,128)} fusion(bf16[512,256]{1,0:T(8,128)(2,1)S(1)} %reshape.96, bf16[64,8,64,128]{3,2,1,0:T(8,128)(2,1)} %bitcast.126), kind=kOutput, calls=%fused_computation.2 | convolution fusion | flops 2147483648 | bytes 17039360 | tf_op jit(solution)/shard_map/dot_general | solution.py:82
  249.2 1.9 convolution_bitcast_fusion
  251.1 1.9 convolution_bitcast_fusion.2
  254.2 30.1 %all-gather.5.cloned.1.call-done = bf16[8192,256]{1,0:T(8,128)(2,1)} async-done(((bf16[512,256]{1,0:T(8,128)(2,1)}), bf16[8192,256]{1,0:T(8,128)(2,1)}) %all-gather.5.cloned.1.call-update) | async-done | bytes 4194320 | tf_op jit(solution)/shard_map/all_gather | solution.py:57
  284.3 9.3 %fusion.16 = bf16[512,256]{1,0:T(8,128)(2,1)S(1)} fusion(bf16[8192,256]{1,0:T(8,128)(2,1)} %all-gather.5.cloned.1.call-done, bf16[64,8,64,128]{3,2,1,0:T(8,128)(2,1)} %bitcast.127), kind=kOutput, calls=%fused_computation.24 | convolution fusion | flops 2147614720 | bytes 12845056 | tf_op jit(solution)/shard_map/dot_general | solution.py:30
  294.6 89.5 %reduce-scatter.5.cloned.1.call-done = f32[512,256]{1,0:T(8,128)} async-done(((f32[8192,256]{1,0:T(8,128)}), f32[512,256]{1,0:T(8,128)}) %reduce-scatter.5.cloned.1.call-update) | async-done | bytes 524304 | tf_op jit(solution)/shard_map/reduce_scatter | solution.py:81
  387.1 1.6 pad_maximum_fusion.7
  388.7 1.6 pad_maximum_fusion.6
  392.7 4.0 collective-permute-start.3
  396.7 130.6 %all-reduce.5.cloned.1.call-done = (f32[2,128,256]{2,1,0:T(8,128)}, f32[2,128,256]{2,1,0:T(8,128)}, f32[2,128,128]{2,1,0:T(8,128)}, f32[2,128,128]{2,1,0:T(8,128)}) async-done(((f32[2,128,256]{2,1,0:T(8,128)}, f32[2,128,256]{2,1,0:T(8,128)}, f32[2,128,128]{2,1,0:T(8,128)}, f32[2,128,128]{2,1,0:T(8,128)}), (f32[2,128,256]{2,1,0:T(8,128)}, f32[2,128,256]{2,1,0:T(8,128)}, f32[2,128,128]{2,1,0:T(8,128)}, ...) | async-done | bytes 786448 | tf_op jit(solution)/shard_map/psum | solution.py:117
  530.5 144.9 %all-reduce.7.cloned.1.call-done = (f32[2,128,256]{2,1,0:T(8,128)}, f32[2,128,256]{2,1,0:T(8,128)}, f32[2,128,128]{2,1,0:T(8,128)}, f32[2,128,128]{2,1,0:T(8,128)}) async-done(((f32[2,128,256]{2,1,0:T(8,128)}, f32[2,128,256]{2,1,0:T(8,128)}, f32[2,128,128]{2,1,0:T(8,128)}, f32[2,128,128]{2,1,0:T(8,128)}), (f32[2,128,256]{2,1,0:T(8,128)}, f32[2,128,256]{2,1,0:T(8,128)}, f32[2,128,128]{2,1,0:T(8,128)}, ...) | async-done | bytes 786448 | tf_op jit(solution)/shard_map/psum | solution.py:116
  675.4 1.7 broadcast_multiply_fusion.2
  677.1 1.9 broadcast_multiply_fusion
  (80 shorter events, 21.0 us)
Async XLA Ops:
  7.2 92.9 %all-gather.3.cloned.1.call-start = ((), (), s32[]{:S(2)}) async-start(), calls=%async_computation.3 | async-start | bytes 4456448 | tf_op jit(solution)/shard_map/all_gather | solution.py:57
  7.2 10.3 %collective-permute-start = (bf16[512,2,128]{2,1,0:T(2,128)(2,1)}, bf16[512,2,128]{2,1,0:T(2,128)(2,1)S(1)}, u32[]{:S(2)}, u32[]{:S(2)}) collective-permute-start(bf16[512,2,128]{2,1,0:T(2,128)(2,1)} %param.9), channel_id=1, source_target_pairs={{0,1},{1,2},{2,3},{3,4},{4,5},{5,6},{6,7},{7,8},{8,9},{9,10},{10,1... | collective-permute-start | bytes 786440 | tf_op jit(solution)/shard_map/ppermute | solution.py:12
  19.4 1.2 copy-start.3
  21.7 179.6 %reduce-scatter.3.cloned.1.call-start = ((), (), s32[]{:S(2)}) async-start(), calls=%async_computation.2 | async-start | bytes 8912896 | tf_op jit(solution)/shard_map/reduce_scatter | solution.py:81
  29.7 12.1 %copy-start = (bf16[512,2,128]{2,1,0:T(2,128)(2,1)S(1)}, bf16[512,2,128]{2,1,0:T(2,128)(2,1)}, u32[]{:S(2)}) copy-start(bf16[512,2,128]{2,1,0:T(2,128)(2,1)} %param.10) | copy-start | bytes 786436
  29.7 12.1 %copy-start.14 = (bf16[2,128,128]{2,1,0:T(8,128)(2,1)S(1)}, bf16[2,128,128]{2,1,0:T(8,128)(2,1)}, u32[]{:S(2)}) copy-start(bf16[2,128,128]{2,1,0:T(8,128)(2,1)} %param.16) | copy-start | bytes 196612
  66.7 0.8 copy-start.15
  66.8 217.5 %all-gather.5.cloned.1.call-start = ((), (), s32[]{:S(2)}) async-start(), calls=%async_computation.5 | async-start | bytes 4456448 | tf_op jit(solution)/shard_map/all_gather | solution.py:57
  67.8 41.9 %copy-start.1 = (bf16[512,2,128]{2,1,0:T(2,128)(2,1)S(1)}, bf16[512,2,128]{2,1,0:T(2,128)(2,1)}, u32[]{:S(2)}) copy-start(bf16[512,2,128]{2,1,0:T(2,128)(2,1)} %param.9) | copy-start | bytes 786436
  67.8 45.4 %copy-start.9 = (bf16[2,128,256]{2,1,0:T(8,128)(2,1)S(1)}, bf16[2,128,256]{2,1,0:T(8,128)(2,1)}, u32[]{:S(2)}) copy-start(bf16[2,128,256]{2,1,0:T(8,128)(2,1)} %param.14) | copy-start | bytes 393220
  67.8 57.7 %copy-start.8 = (bf16[2,128,256]{2,1,0:T(8,128)(2,1)S(1)}, bf16[2,128,256]{2,1,0:T(8,128)(2,1)}, u32[]{:S(2)}) copy-start(bf16[2,128,256]{2,1,0:T(8,128)(2,1)} %param.13) | copy-start | bytes 393220
  110.0 13.9 %collective-permute-start.1 = (bf16[512,2,128]{2,1,0:T(2,128)(2,1)S(1)}, bf16[512,2,128]{2,1,0:T(2,128)(2,1)S(1)}, u32[]{:S(2)}, u32[]{:S(2)}) collective-permute-start(bf16[512,2,128]{2,1,0:T(2,128)(2,1)S(1)} %add_convert_fusion), channel_id=1, source_target_pairs={{0,1},{1,2},{2,3},{3,4},{4,5},{5,6},{6,7},{7,8},{8,9},{9,10},{10,1... | collective-permute-start | bytes 786440 | tf_op jit(solution)/shard_map/ppermute | solution.py:12
  124.8 0.7 copy-start.5
  207.3 176.8 %reduce-scatter.5.cloned.1.call-start = ((), (), s32[]{:S(2)}) async-start(), calls=%async_computation.4 | async-start | bytes 8912896 | tf_op jit(solution)/shard_map/reduce_scatter | solution.py:81
  209.7 10.6 %collective-permute-start.2 = (f32[512,2,128]{2,0,1:T(8,128)S(1)}, f32[512,2,128]{2,0,1:T(8,128)}, u32[]{:S(2)}, u32[]{:S(2)}) collective-permute-start(f32[512,2,128]{2,0,1:T(8,128)S(1)} %fusion.33), channel_id=1, source_target_pairs={{1,0},{2,1},{3,2},{4,3},{5,4},{6,5},{7,6},{8,7},{9,8},{10,9},{11,1... | collective-permute-start | bytes 1572872 | tf_op jit(solution)/shard_map/ppermute | solution.py:12
  248.0 1.0 copy-start.7
  248.0 1.2 copy-start.11
  248.0 3.1 copy-start.6
  248.0 279.3 %all-reduce.5.cloned.1.call-start = ((), (), s32[]{:S(2)}) async-start(), calls=%async_computation.6 | async-start | bytes 1572864 | tf_op jit(solution)/shard_map/psum | solution.py:117
  254.2 132.5 %copy-start.4 = (bf16[512,2,128]{2,1,0:T(2,128)(2,1)S(1)}, bf16[512,2,128]{2,1,0:T(2,128)(2,1)}, u32[]{:S(2)}) copy-start(bf16[512,2,128]{2,1,0:T(2,128)(2,1)} %copy-done.3) | copy-start | bytes 786436
  293.6 235.4 %copy-start.2 = (f32[512,2,128]{2,0,1:T(8,128)S(1)}, f32[512,2,128]{2,0,1:T(8,128)}, u32[]{:S(2)}) copy-start(f32[512,2,128]{2,0,1:T(8,128)} %get-tuple-element.31) | copy-start | bytes 1572868
  293.6 235.4 %copy-start.10 = (bf16[2,128,256]{2,1,0:T(8,128)(2,1)S(1)}, bf16[2,128,256]{2,1,0:T(8,128)(2,1)}, u32[]{:S(2)}) copy-start(bf16[2,128,256]{2,1,0:T(8,128)(2,1)} %param.14) | copy-start | bytes 393220
  386.3 0.7 copy-start.13
  386.4 4.0 copy-start.12
  390.3 285.1 %all-reduce.7.cloned.1.call-start = ((), (), s32[]{:S(2)}) async-start(), calls=%async_computation.7 | async-start | bytes 1572864 | tf_op jit(solution)/shard_map/psum | solution.py:116
  392.7 136.3 %collective-permute-start.3 = (f32[512,2,128]{2,0,1:T(8,128)S(1)}, f32[512,2,128]{2,0,1:T(8,128)S(1)}, u32[]{:S(2)}, u32[]{:S(2)}) collective-permute-start(f32[512,2,128]{2,0,1:T(8,128)S(1)} %fusion.30), channel_id=1, source_target_pairs={{1,0},{2,1},{3,2},{4,3},{5,4},{6,5},{7,6},{8,7},{9,8},{10,9},{11,1... | collective-permute-start | bytes 1572872 | tf_op jit(solution)/shard_map/ppermute | solution.py:12
Sparse Core Ops, SparseCore 0:
  21.8 78.2 all-gather.2
  102.6 98.6 reduce-scatter.2
  207.4 76.7 all-gather.4
  286.7 97.3 reduce-scatter.4
  390.5 136.7 all-reduce.4
  530.0 145.4 all-reduce.6
